TPU v7x, 32 devices: a whole 2x2x4 slice. The times are simulated.
32 devices in a mesh: seq: 16 (over z, y, core), dp: 2 (over x).
Axes of the slice: x: 2, y: 2, z: 4, core: 2. Of those that a mesh axis runs over, the one named last changes fastest.
Arguments:
- queries: bfloat16 [2, 4096, 2048], P('dp', 'seq'), may hold values from -6 to 6
- key_rows: bfloat16 [2, 4096, 2048], P('dp', 'seq'), may hold values from -6 to 6
- value_rows: bfloat16 [2, 4096, 2048], P('dp', 'seq'), may hold values from -6 to 6
- out_grad: bfloat16 [2, 4096, 2048], P('dp', 'seq'), may hold values from -6 to 6
- out_weight: bfloat16 [2048, 2048], P('seq', 'dp'), may hold values from -0.125 to 0.125
Outputs:
- query_grad: bfloat16 [2, 4096, 2048], P('dp', 'seq')
- key_grad: bfloat16 [2, 4096, 2048], P('dp', 'seq')
- value_grad: bfloat16 [2, 4096, 2048], P('dp', 'seq')
- weight_grad: float32 [2048, 2048], P('seq', 'dp')
All inputs are finite; a program needn't handle non-finite values.
Results may differ from a plain program's by a relative error of at most 0.014.
Values may be sent and summed in bfloat16 or wider, within the bound.
A program may use at most 192 MiB of HBM per device.

v0:
```python
import math
import jax
import jax.numpy as jnp
from jax import lax
from jax.sharding import PartitionSpec as P

HEADS = 16
HEAD = 128
HD = 2048


def exchanged_sums(part, scale, axis, reverse):
    count = lax.axis_size(axis)
    heads, depth, width = part.shape
    rows = part.reshape(heads * depth, width).astype(jnp.bfloat16)
    mine = lax.all_to_all(rows, axis, 0, 0, tiled=True)
    mine = mine.reshape(count, -1, width).astype(jnp.float32)
    order = range(count - 1, -1, -1) if reverse else range(count)
    state = jnp.zeros_like(mine[0])
    sums = [None] * count
    for source in order:
        sums[source] = (scale * state).astype(jnp.bfloat16)
        state = state + mine[source]
    back = lax.all_to_all(jnp.concatenate(sums, axis=0), axis, 0, 0, tiled=True)
    return back.reshape(heads, depth, width)


def shards(queries, key_rows, value_rows, out_grad, out_weight):
    tokens_dev = queries.shape[1]
    seq_devices = lax.axis_size("seq")
    data_devices = lax.axis_size("dp")
    seq_length = tokens_dev * seq_devices
    seq_count = queries.shape[0] * data_devices
    score_scale = 1.0 / math.sqrt(HEAD * seq_length)
    grad_scale = 1.0 / math.sqrt(seq_count * seq_length)
    query_flat = queries[0]
    grad_flat = out_grad[0]
    query_h = query_flat.reshape(tokens_dev, HEADS, HEAD)
    key_h = key_rows[0].reshape(tokens_dev, HEADS, HEAD)
    value_h = value_rows[0].reshape(tokens_dev, HEADS, HEAD)
    row_ids = lax.broadcasted_iota(jnp.int32, (tokens_dev, tokens_dev), 0)
    col_ids = lax.broadcasted_iota(jnp.int32, (tokens_dev, tokens_dev), 1)
    causal = (row_ids >= col_ids).astype(jnp.float32)
    kv_local = jnp.einsum("shd,she->hde", key_h, value_h, preferred_element_type=jnp.float32)
    wide_weight = lax.all_gather(out_weight, "dp", axis=1, tiled=True)
    head_grad = lax.dot_general(
        grad_flat,
        lax.all_gather(wide_weight, "seq", axis=0, tiled=True),
        (((1,), (1,)), ((), ())),
        preferred_element_type=jnp.float32,
    ).astype(jnp.bfloat16)
    grad_h = head_grad.reshape(tokens_dev, HEADS, HEAD)
    query_dout = jnp.einsum("thd,the->hde", query_h, grad_h, preferred_element_type=jnp.float32)
    prefix_scaled = exchanged_sums(kv_local, score_scale, "seq", False)
    suffix_scaled = exchanged_sums(query_dout, score_scale, "seq", True)
    scores = (
        score_scale
        * jnp.einsum("thd,shd->hts", query_h, key_h, preferred_element_type=jnp.float32)
        * causal
    ).astype(jnp.bfloat16)
    attended = jnp.einsum("hts,shd->thd", scores, value_h, preferred_element_type=jnp.float32)
    attended = attended + jnp.einsum(
        "thd,hde->the", query_h, prefix_scaled, preferred_element_type=jnp.float32
    )
    attended = attended.astype(jnp.bfloat16).reshape(tokens_dev, HD)
    row_sums = lax.psum_scatter(
        (
            grad_scale
            * lax.dot_general(
                attended, grad_flat, (((0,), (0,)), ((), ())), preferred_element_type=jnp.float32
            )
        ).astype(jnp.bfloat16),
        "seq",
        scatter_dimension=0,
        tiled=True,
    )
    weight_grad = lax.psum_scatter(row_sums, "dp", scatter_dimension=1, tiled=True).astype(
        jnp.float32
    )
    grad_scores = (
        score_scale
        * jnp.einsum("the,she->hts", grad_h, value_h, preferred_element_type=jnp.float32)
        * causal
    ).astype(jnp.bfloat16)
    query_g = jnp.einsum("hts,shd->thd", grad_scores, key_h, preferred_element_type=jnp.float32)
    query_g = query_g + jnp.einsum(
        "the,hde->thd", grad_h, prefix_scaled, preferred_element_type=jnp.float32
    )
    key_g = jnp.einsum("hts,thd->shd", grad_scores, query_h, preferred_element_type=jnp.float32)
    key_g = key_g + jnp.einsum(
        "she,hde->shd", value_h, suffix_scaled, preferred_element_type=jnp.float32
    )
    value_g = jnp.einsum("hts,the->she", scores, grad_h, preferred_element_type=jnp.float32)
    value_g = value_g + jnp.einsum(
        "shd,hde->she", key_h, suffix_scaled, preferred_element_type=jnp.float32
    )
    query_grad = query_g.astype(jnp.bfloat16).reshape(1, tokens_dev, HD)
    key_grad = key_g.astype(jnp.bfloat16).reshape(1, tokens_dev, HD)
    value_grad = value_g.astype(jnp.bfloat16).reshape(1, tokens_dev, HD)
    return (query_grad, key_grad, value_grad, weight_grad)


def solution(mesh):
    return jax.shard_map(
        shards,
        mesh=mesh,
        in_specs=(
            P("dp", "seq", None),
            P("dp", "seq", None),
            P("dp", "seq", None),
            P("dp", "seq", None),
            P("seq", "dp"),
        ),
        out_specs=(
            P("dp", "seq", None),
            P("dp", "seq", None),
            P("dp", "seq", None),
            P("seq", "dp"),
        ),
        check_vma=False,
    )
```

profile of v0, /device:TPU:0, one launch (start us, length us, event | category | flops | bytes accessed | tf_op | source)
XLA Modules:
  0.0 319.2 jit_solution(4573787005507438147)
XLA Ops:
  7.2 1.5 copy.36
  8.7 1.5 copy.35
  10.2 1.3 convolution_convert_fusion.2
  11.5 7.4 %all-to-all-start = ((bf16[16,128,128]{2,1,0:T(8,128)(2,1)}), bf16[16,128,128]{2,1,0:T(8,128)(2,1)}, u32[]{:S(2)}, u32[]{:S(2)}) async-start(bf16[16,128,128]{2,1,0:T(8,128)(2,1)} %convolution_convert_fusion.2), calls=%async_computation | async-start | bytes 1048576 | tf_op jit(solution)/shard_map/all_to_all | solution.py:16
  19.6 13.9 %all-to-all-done = bf16[16,128,128]{2,1,0:T(8,128)(2,1)} async-done(((bf16[16,128,128]{2,1,0:T(8,128)(2,1)}), bf16[16,128,128]{2,1,0:T(8,128)(2,1)}, u32[]{:S(2)}, u32[]{:S(2)}) %all-to-all-start) | async-done | bytes 524320 | tf_op jit(solution)/shard_map/all_to_all | solution.py:16
  33.5 1.1 convert_element_type.159
  34.6 0.6 constant_dynamic-update-slice_fusion.14
  35.2 0.6 constant_dynamic-update-slice_fusion.13
  35.9 0.6 constant_dynamic-update-slice_fusion.12
  36.5 0.6 constant_dynamic-update-slice_fusion.11
  37.7 0.6 constant_dynamic-update-slice_fusion.9
  39.0 0.6 constant_dynamic-update-slice_fusion.7
  40.3 0.6 constant_dynamic-update-slice_fusion.5
  41.5 0.6 constant_dynamic-update-slice_fusion.3
  42.8 0.6 constant_dynamic-update-slice_fusion.1
  43.4 0.6 constant_dynamic-update-slice_fusion
  44.0 4.2 %all-to-all-start.1 = ((bf16[16,128,128]{2,1,0:T(8,128)(2,1)}), bf16[16,128,128]{2,1,0:T(8,128)(2,1)}, u32[]{:S(2)}, u32[]{:S(2)}) async-start(bf16[16,128,128]{2,1,0:T(8,128)(2,1)} %bitcast.201), calls=%async_computation.1 | async-start | bytes 1048576 | tf_op jit(solution)/shard_map/all_to_all | solution.py:24
  48.3 1.5 copy.37
  49.8 0.7 multiply_convert_fusion.1
  50.8 1.3 copy-done.3
  52.1 2.2 fusion.52
  54.3 8.4 %all-to-all-done.1 = bf16[16,128,128]{2,1,0:T(8,128)(2,1)} async-done(((bf16[16,128,128]{2,1,0:T(8,128)(2,1)}), bf16[16,128,128]{2,1,0:T(8,128)(2,1)}, u32[]{:S(2)}, u32[]{:S(2)}) %all-to-all-start.1) | async-done | bytes 524320 | tf_op jit(solution)/shard_map/all_to_all | solution.py:24
  62.7 2.6 fusion
  65.3 5.6 %multiply_convert_fusion = bf16[2048,2048]{1,0:T(8,128)(2,1)} fusion(bf16[256,2048]{0,1:T(8,128)(2,1)S(1)} %bitcast.200, bf16[1,256,2048]{2,1,0:T(8,128)(2,1)S(1)} %copy-done), kind=kOutput, calls=%fused_computation | convolution fusion | flops 2155872256 | bytes 10485760 | tf_op jit(solution)/shard_map/dot_general | solution.py:69
  71.0 10.6 %all_gather.6 = bf16[128,2048]{1,0:T(8,128)(2,1)} all-gather(bf16[128,1024]{1,0:T(8,128)(2,1)} %param.9), channel_id=1, replica_groups=mesh['seq'=16,'dp'=2] {'dp'}, dimensions={1}, use_global_device_ids=true | all-gather | bytes 786432 | tf_op jit(solution)/shard_map/all_gather | solution.py:45
  81.7 93.4 %reduce-scatter.3.cloned.1.call-done = bf16[128,2048]{1,0:T(8,128)(2,1)} async-done(((bf16[2048,2048]{1,0:T(8,128)(2,1)}), bf16[128,2048]{1,0:T(8,128)(2,1)}) %reduce-scatter.3.cloned.1.call-update) | async-done | bytes 524304 | tf_op jit(solution)/shard_map/reduce_scatter | solution.py:66
  175.1 76.8 %all-gather.2.cloned.1.call-done = bf16[2048,2048]{1,0:T(8,128)(2,1)} async-done(((bf16[128,2048]{1,0:T(8,128)(2,1)}), bf16[2048,2048]{1,0:T(8,128)(2,1)}) %all-gather.2.cloned.1.call-update) | async-done | bytes 8388624 | tf_op jit(solution)/shard_map/all_gather | solution.py:48
  251.9 6.7 %convolution_convert_fusion = bf16[256,2048]{1,0:T(8,128)(2,1)} fusion(bf16[2048,2048]{1,0:T(8,128)(2,1)} %all-gather.2.cloned.1.call-done, bf16[1,256,2048]{2,1,0:T(8,128)(2,1)S(1)} %copy-done), kind=kOutput, calls=%fused_computation.3 | convolution fusion | flops 2148007936 | bytes 10485760 | tf_op jit(solution)/shard_map/dot_general | solution.py:46
  258.6 2.3 copy.34
  260.9 2.8 fusion.3
  263.7 4.3 %all-to-all-start.2 = ((bf16[16,128,128]{2,1,0:T(8,128)(2,1)}), bf16[16,128,128]{2,1,0:T(8,128)(2,1)}, u32[]{:S(2)}, u32[]{:S(2)}) async-start(bf16[16,128,128]{2,1,0:T(8,128)(2,1)} %fusion.3), calls=%async_computation.2 | async-start | bytes 1048576 | tf_op jit(solution)/shard_map/all_to_all | solution.py:16
  268.0 1.8 convert_element_type.204
  269.8 2.0 multiply_convert_fusion.2
  271.8 1.3 copy-done.4
  273.1 2.1 fusion.7
  275.2 7.2 %all-to-all-done.2 = bf16[16,128,128]{2,1,0:T(8,128)(2,1)} async-done(((bf16[16,128,128]{2,1,0:T(8,128)(2,1)}), bf16[16,128,128]{2,1,0:T(8,128)(2,1)}, u32[]{:S(2)}, u32[]{:S(2)}) %all-to-all-start.2) | async-done | bytes 524320 | tf_op jit(solution)/shard_map/all_to_all | solution.py:16
  282.4 1.1 convert_element_type.180
  284.0 0.8 copy-done.6
  284.8 4.4 %all-to-all-start.3 = ((bf16[16,128,128]{2,1,0:T(8,128)(2,1)}), bf16[16,128,128]{2,1,0:T(8,128)(2,1)}, u32[]{:S(2)}, u32[]{:S(2)}) async-start(bf16[16,128,128]{2,1,0:T(8,128)(2,1)} %bitcast.202), calls=%async_computation.3 | async-start | bytes 1048576 | tf_op jit(solution)/shard_map/all_to_all | solution.py:24
  289.3 3.5 %fusion.2 = bf16[256,16,128]{0,2,1:T(8,128)(2,1)} fusion(f32[16,256,128]{1,2,0:T(8,128)} %fusion.7, bf16[16,128,128]{2,1,0:T(8,128)(2,1)} %all-to-all-done.1, bf16[256,16,128]{0,2,1:T(8,128)(2,1)} %bitcast.193), kind=kOutput, calls=%fused_computation.9 | convolution fusion | flops 135266304 | bytes 4718592 | tf_op jit(solution)/shard_map/the,hde->thd/dot_general | solution.py:86
  292.7 2.3 copy.28
  295.0 3.8 %fusion.51 = f32[16,128,256]{2,1,0:T(8,128)} fusion(bf16[256,16,128]{0,2,1:T(8,128)(2,1)} %bitcast.194, bf16[16,256,256]{2,1,0:T(8,128)(2,1)} %copy-done.3), kind=kOutput, calls=%fused_computation.150 | convolution fusion | flops 268435456 | bytes 5242880 | tf_op jit(solution)/shard_map/hts,the->she/dot_general | solution.py:93
  298.8 1.9 fusion.11
  300.7 2.8 all-to-all-done.3
  303.5 3.2 %add_convert_fusion = bf16[16,128,256]{2,1,0:T(8,128)(2,1)} fusion(f32[16,128,256]{2,1,0:T(8,128)} %fusion.51, bf16[16,128,128]{2,1,0:T(8,128)(2,1)} %all-to-all-done.3, bf16[256,16,128]{2,1,0:T(8,128)(2,1)S(1)} %bitcast.186), kind=kOutput, calls=%fused_computation.10 | convolution fusion | flops 135266304 | bytes 4718592 | tf_op jit(solution)/shard_map/shd,hde->she/dot_general | solution.py:94
  306.8 2.3 copy.30
  309.1 2.2 fusion.1
  311.3 1.4 copy.29
  (41 shorter events, 4.6 us)
Async XLA Ops:
  7.2 58.2 %copy-start = (bf16[1,256,2048]{2,1,0:T(8,128)(2,1)S(1)}, bf16[1,256,2048]{2,1,0:T(8,128)(2,1)}, u32[]{:S(2)}) copy-start(bf16[1,256,2048]{2,1,0:T(8,128)(2,1)} %param.8) | copy-start | bytes 3145732
  11.5 22.0 %all-to-all-start = ((bf16[16,128,128]{2,1,0:T(8,128)(2,1)}), bf16[16,128,128]{2,1,0:T(8,128)(2,1)}, u32[]{:S(2)}, u32[]{:S(2)}) async-start(bf16[16,128,128]{2,1,0:T(8,128)(2,1)} %convolution_convert_fusion.2), calls=%async_computation | async-start | bytes 1048576 | tf_op jit(solution)/shard_map/all_to_all | solution.py:16
  44.0 18.7 %all-to-all-start.1 = ((bf16[16,128,128]{2,1,0:T(8,128)(2,1)}), bf16[16,128,128]{2,1,0:T(8,128)(2,1)}, u32[]{:S(2)}, u32[]{:S(2)}) async-start(bf16[16,128,128]{2,1,0:T(8,128)(2,1)} %bitcast.201), calls=%async_computation.1 | async-start | bytes 1048576 | tf_op jit(solution)/shard_map/all_to_all | solution.py:24
  48.3 126.8 %reduce-scatter.3.cloned.1.call-start = ((), (), s32[]{:S(2)}) async-start(), calls=%async_computation.7 | async-start | bytes 8912896 | tf_op jit(solution)/shard_map/reduce_scatter | solution.py:66
  49.8 1.0 copy-start.1
  50.8 1.3 copy-start.3
  70.9 181.0 %all-gather.2.cloned.1.call-start = ((), (), s32[]{:S(2)}) async-start(), calls=%async_computation.6 | async-start | bytes 8912896 | tf_op jit(solution)/shard_map/all_gather | solution.py:48
  81.7 186.3 %reduce-scatter.5.cloned.1.call-start = ((), (), s32[]{:S(2)}) async-start(), calls=%async_computation.8 | async-start | bytes 786432 | tf_op jit(solution)/shard_map/reduce_scatter | solution.py:77
  263.7 18.7 %all-to-all-start.2 = ((bf16[16,128,128]{2,1,0:T(8,128)(2,1)}), bf16[16,128,128]{2,1,0:T(8,128)(2,1)}, u32[]{:S(2)}, u32[]{:S(2)}) async-start(bf16[16,128,128]{2,1,0:T(8,128)(2,1)} %fusion.3), calls=%async_computation.2 | async-start | bytes 1048576 | tf_op jit(solution)/shard_map/all_to_all | solution.py:16
  271.8 1.3 copy-start.4
  284.0 0.8 copy-start.6
  284.8 18.7 %all-to-all-start.3 = ((bf16[16,128,128]{2,1,0:T(8,128)(2,1)}), bf16[16,128,128]{2,1,0:T(8,128)(2,1)}, u32[]{:S(2)}, u32[]{:S(2)}) async-start(bf16[16,128,128]{2,1,0:T(8,128)(2,1)} %bitcast.202), calls=%async_computation.3 | async-start | bytes 1048576 | tf_op jit(solution)/shard_map/all_to_all | solution.py:24
  295.0 3.8 %copy-start.2 = (bf16[32,8,16,128]{3,2,1,0:T(8,128)(2,1)S(1)}, bf16[32,8,16,128]{3,2,1,0:T(8,128)(2,1)}, u32[]{:S(2)}) copy-start(bf16[32,8,16,128]{3,2,1,0:T(8,128)(2,1)} %copy-done.1) | copy-start | bytes 3145732
  295.0 3.8 %copy-start.5 = (bf16[16,256,256]{2,1,0:T(8,128)(2,1)S(1)}, bf16[16,256,256]{2,1,0:T(8,128)(2,1)}, u32[]{:S(2)}) copy-start(bf16[16,256,256]{2,1,0:T(8,128)(2,1)} %copy-done.4) | copy-start | bytes 6291460
Sparse Core Ops, SparseCore 0:
  71.1 103.9 reduce-scatter.2
  177.2 74.6 all-gather.1
  254.2 12.7 reduce-scatter.4
where the time goes:
time: 320 us; the launch traced here: 319 us
  waiting for transfers between devices  203 us (63%)
  matrix products  40.6 us (13%)
  starting transfers between devices  20.5 us (6%)
  local copies, waits for them, and re-layouts  17 us (5%)
  between operations  14 us (4%)
  other arithmetic  13.8 us (4%)
  blocking collectives  10.6 us (3%)
    reduce_scatter x1, waiting for transfers between devices, shards(): lax.psum_scatter((grad_scale * lax.dot_general(attended, grad_flat, (((0,...  93.4 us
    all_gather x1, waiting for transfers between devices, shards(): lax.all_gather(wide_weight, 'seq', axis=0, tiled=True)  76.8 us
    all_to_all x2, waiting for transfers between devices, exchanged_sums(): mine = lax.all_to_all(rows, axis, 0, 0, tiled=True)  21.1 us
    unnamed x20, local copies, waits for them, and re-layouts  13.3 us
    all_to_all x2, starting transfers between devices, exchanged_sums(): mine = lax.all_to_all(rows, axis, 0, 0, tiled=True)  11.7 us
    all_to_all x2, waiting for transfers between devices, exchanged_sums(): back = lax.all_to_all(jnp.concatenate(sums, axis=0), axis, 0, 0, tiled=True)  11.3 us
    all_gather x1, blocking collectives, shards(): wide_weight = lax.all_gather(out_weight, 'dp', axis=1, tiled=True)  10.6 us
    unnamed x29, other arithmetic  9.13 us
  transfers between devices with their start and end apart: 7, of which 6 were waited for; matrix products, arithmetic and copies ran while one was open for 11% of the time, Pallas kernels for 0%

commit v1 on v0

--- a/solution.py
+++ b/solution.py
@@ -7,6 +7,19 @@
 HEADS = 16
 HEAD = 128
 HD = 2048
+
+
+def collect(x, axis, dim):
+    ways = lax.axis_size(axis)
+    up = [(d, (d + 1) % ways) for d in range(ways)]
+    down = [(d, (d - 1) % ways) for d in range(ways)]
+    earlier, later = ([x], [x])
+    for _ in range(ways // 2):
+        earlier.append(lax.ppermute(earlier[-1], axis, up))
+    for _ in range((ways - 1) // 2):
+        later.append(lax.ppermute(later[-1], axis, down))
+    line = jnp.concatenate([*earlier[::-1], *later[1:]], axis=dim)
+    return jnp.roll(line, (lax.axis_index(axis) - ways // 2) * x.shape[dim], axis=dim)
 
 
 def exchanged_sums(part, scale, axis, reverse):
@@ -45,7 +58,7 @@
     wide_weight = lax.all_gather(out_weight, "dp", axis=1, tiled=True)
     head_grad = lax.dot_general(
         grad_flat,
-        lax.all_gather(wide_weight, "seq", axis=0, tiled=True),
+        collect(wide_weight, "seq", 0),
         (((1,), (1,)), ((), ())),
         preferred_element_type=jnp.float32,
     ).astype(jnp.bfloat16)

time: 320 us -> 284 us (0.89)
  waiting for transfers between devices: 203 us -> 81.3 us
  starting transfers between devices: 20.5 us -> 75.6 us
  local copies, waits for them, and re-layouts: 17 us -> 43.8 us
    all_gather x1 -> x0, waiting for transfers between devices: 76.8 us -> none  [shards(): lax.all_gather(wide_weight, 'seq', axis=0, tiled=True)]
    reduce_scatter x1, waiting for transfers between devices: 93.4 us -> 36.6 us  [shards(): lax.psum_scatter((grad_scale * lax.dot_general(attended, grad_flat, (((0,...]
    ppermute x0 -> x15, starting transfers between devices: none -> 43.2 us  [the longest x7 21.7 us: collect(): later.append(lax.ppermute(later[-1], axis, down))]
    unnamed x20 -> x59, local copies, waits for them, and re-layouts: 13.3 us -> 42.3 us
    ppermute x0 -> x15, waiting for transfers between devices: none -> 28.6 us  [the longest x8 25.2 us: collect(): earlier.append(lax.ppermute(earlier[-1], axis, up))]
    all_to_all x2, waiting for transfers between devices: 11.3 us -> 0.01 us  [exchanged_sums(): back = lax.all_to_all(jnp.concatenate(sums, axis=0), axis, 0, 0, tiled=True)]
    all_to_all x2, starting transfers between devices: 8.67 us -> 18.3 us  [exchanged_sums(): back = lax.all_to_all(jnp.concatenate(sums, axis=0), axis, 0, 0, tiled=True)]
    all_to_all x2, waiting for transfers between devices: 21.1 us -> 16.1 us  [exchanged_sums(): mine = lax.all_to_all(rows, axis, 0, 0, tiled=True)]
  transfers between devices with their start and end apart: 7 -> 21, of which waited for: 6 -> 9; matrix products, arithmetic and copies ran while one was open for 11% -> 33% of each run, Pallas kernels for 0% -> 0%
where the time goes in v1:
time: 284 us; the launch traced here: 281 us
  waiting for transfers between devices  81.3 us (29%)
  starting transfers between devices  75.6 us (27%)
  local copies, waits for them, and re-layouts  43.8 us (15%)
  matrix products  42.8 us (15%)
  between operations  14.5 us (5%)
  other arithmetic  13.9 us (5%)
  blocking collectives  9.45 us (3%)
    unnamed x59, local copies, waits for them, and re-layouts  42.3 us
    reduce_scatter x1, waiting for transfers between devices, shards(): lax.psum_scatter((grad_scale * lax.dot_general(attended, grad_flat, (((0,...  36.6 us
    ppermute x8, waiting for transfers between devices, collect(): earlier.append(lax.ppermute(earlier[-1], axis, up))  25.2 us
    ppermute x7, starting transfers between devices, collect(): later.append(lax.ppermute(later[-1], axis, down))  21.7 us
    ppermute x8, starting transfers between devices, collect(): earlier.append(lax.ppermute(earlier[-1], axis, up))  21.5 us
    all_to_all x2, starting transfers between devices, exchanged_sums(): back = lax.all_to_all(jnp.concatenate(sums, axis=0), axis, 0, 0, tiled=True)  18.3 us
    all_to_all x2, waiting for transfers between devices, exchanged_sums(): mine = lax.all_to_all(rows, axis, 0, 0, tiled=True)  16.1 us
    all_to_all x2, starting transfers between devices, exchanged_sums(): mine = lax.all_to_all(rows, axis, 0, 0, tiled=True)  14 us
  transfers between devices with their start and end apart: 21, of which 9 were waited for; matrix products, arithmetic and copies ran while one was open for 33% of the time, Pallas kernels for 0%

profile of v1, /device:TPU:0, one launch (start us, length us, event | category | flops | bytes accessed | tf_op | source)
XLA Modules:
  0.0 281.3 jit_solution(15027212511141080659)
XLA Ops:
  7.2 1.5 copy.35
  8.7 1.5 copy.34
  10.2 1.3 convolution_convert_fusion.1
  11.5 7.4 %all-to-all-start = ((bf16[16,128,128]{2,1,0:T(8,128)(2,1)}), bf16[16,128,128]{2,1,0:T(8,128)(2,1)}, u32[]{:S(2)}, u32[]{:S(2)}) async-start(bf16[16,128,128]{2,1,0:T(8,128)(2,1)} %convolution_convert_fusion.1), calls=%async_computation | async-start | bytes 1048576 | tf_op jit(solution)/shard_map/all_to_all | solution.py:29
  18.9 9.4 %all_gather.3 = bf16[128,2048]{1,0:T(8,128)(2,1)S(1)} all-gather(bf16[128,1024]{1,0:T(8,128)(2,1)} %param.9), channel_id=1, replica_groups=mesh['seq'=16,'dp'=2] {'dp'}, dimensions={1}, use_global_device_ids=true | all-gather | bytes 786432 | tf_op jit(solution)/shard_map/all_gather | solution.py:58
  29.2 3.7 %collective-permute-start.8 = (bf16[128,2048]{1,0:T(8,128)(2,1)S(1)}, bf16[128,2048]{1,0:T(8,128)(2,1)}, u32[]{:S(2)}, u32[]{:S(2)}) collective-permute-start(bf16[128,2048]{1,0:T(8,128)(2,1)S(1)} %all_gather.3), channel_id=1, source_target_pairs={{0,30},{2,0},{4,2},{6,4},{8,6},{10,8},{12,10},{14,12},{16,14},{18,... | collective-permute-start | bytes 1572872 | tf_op jit(solution)/shard_map/ppermute | solution.py:20
  33.5 6.5 %collective-permute-done = bf16[128,2048]{1,0:T(8,128)(2,1)} collective-permute-done((bf16[128,2048]{1,0:T(8,128)(2,1)S(1)}, bf16[128,2048]{1,0:T(8,128)(2,1)}, u32[]{:S(2)}, u32[]{:S(2)}) %collective-permute-start) | collective-permute-done | bytes 524320 | tf_op jit(solution)/shard_map/ppermute | solution.py:18
  40.0 2.7 collective-permute-start.1
  42.6 1.8 collective-permute-start.9
  48.1 3.6 %collective-permute-done.1 = bf16[128,2048]{1,0:T(8,128)(2,1)} collective-permute-done((bf16[128,2048]{1,0:T(8,128)(2,1)}, bf16[128,2048]{1,0:T(8,128)(2,1)}, u32[]{:S(2)}, u32[]{:S(2)}) %collective-permute-start.1) | collective-permute-done | bytes 524320 | tf_op jit(solution)/shard_map/ppermute | solution.py:18
  51.7 4.6 %collective-permute-start.2 = (bf16[128,2048]{1,0:T(8,128)(2,1)}, bf16[128,2048]{1,0:T(8,128)(2,1)S(1)}, u32[]{:S(2)}, u32[]{:S(2)}) collective-permute-start(bf16[128,2048]{1,0:T(8,128)(2,1)} %collective-permute-done.1), channel_id=1, source_target_pairs={{0,2},{2,4},{4,6},{6,8},{8,10},{10,12},{12,14},{14,16},{16,18},{18... | collective-permute-start | bytes 1572872 | tf_op jit(solution)/shard_map/ppermute | solution.py:18
  58.2 5.0 %collective-permute-done.2 = bf16[128,2048]{1,0:T(8,128)(2,1)S(1)} collective-permute-done((bf16[128,2048]{1,0:T(8,128)(2,1)}, bf16[128,2048]{1,0:T(8,128)(2,1)S(1)}, u32[]{:S(2)}, u32[]{:S(2)}) %collective-permute-start.2) | collective-permute-done | bytes 524320 | tf_op jit(solution)/shard_map/ppermute | solution.py:18
  63.2 2.0 collective-permute-start.3
  67.1 2.4 collective-permute-start.10
  69.5 5.1 %collective-permute-done.3 = bf16[128,2048]{1,0:T(8,128)(2,1)S(1)} collective-permute-done((bf16[128,2048]{1,0:T(8,128)(2,1)S(1)}, bf16[128,2048]{1,0:T(8,128)(2,1)S(1)}, u32[]{:S(2)}, u32[]{:S(2)}) %collective-permute-start.3) | collective-permute-done | bytes 524320 | tf_op jit(solution)/shard_map/ppermute | solution.py:18
  74.6 4.7 %collective-permute-start.4 = (bf16[128,2048]{1,0:T(8,128)(2,1)S(1)}, bf16[128,2048]{1,0:T(8,128)(2,1)}, u32[]{:S(2)}, u32[]{:S(2)}) collective-permute-start(bf16[128,2048]{1,0:T(8,128)(2,1)S(1)} %collective-permute-done.3), channel_id=1, source_target_pairs={{0,2},{2,4},{4,6},{6,8},{8,10},{10,12},{12,14},{14,16},{16,18},{18... | collective-permute-start | bytes 1572872 | tf_op jit(solution)/shard_map/ppermute | solution.py:18
  81.3 4.8 %collective-permute-done.4 = bf16[128,2048]{1,0:T(8,128)(2,1)} collective-permute-done((bf16[128,2048]{1,0:T(8,128)(2,1)S(1)}, bf16[128,2048]{1,0:T(8,128)(2,1)}, u32[]{:S(2)}, u32[]{:S(2)}) %collective-permute-start.4) | collective-permute-done | bytes 524320 | tf_op jit(solution)/shard_map/ppermute | solution.py:18
  86.0 7.5 %collective-permute-start.5 = (bf16[128,2048]{1,0:T(8,128)(2,1)}, bf16[128,2048]{1,0:T(8,128)(2,1)}, u32[]{:S(2)}, u32[]{:S(2)}) collective-permute-start(bf16[128,2048]{1,0:T(8,128)(2,1)} %collective-permute-done.4), channel_id=1, source_target_pairs={{0,2},{2,4},{4,6},{6,8},{8,10},{10,12},{12,14},{14,16},{16,18},{18... | collective-permute-start | bytes 1572872 | tf_op jit(solution)/shard_map/ppermute | solution.py:18
  94.8 7.2 %all-to-all-start.1 = ((bf16[16,128,128]{2,1,0:T(8,128)(2,1)}), bf16[16,128,128]{2,1,0:T(8,128)(2,1)}, u32[]{:S(2)}, u32[]{:S(2)}) async-start(bf16[16,128,128]{2,1,0:T(8,128)(2,1)} %bitcast.202), calls=%async_computation.1 | async-start | bytes 1048576 | tf_op jit(solution)/shard_map/all_to_all | solution.py:37
  102.1 1.5 copy.36
  103.6 4.4 %collective-permute-start.12 = (bf16[128,2048]{1,0:T(8,128)(2,1)}, bf16[128,2048]{1,0:T(8,128)(2,1)}, u32[]{:S(2)}, u32[]{:S(2)}) collective-permute-start(bf16[128,2048]{1,0:T(8,128)(2,1)} %collective-permute-done.11), channel_id=1, source_target_pairs={{0,30},{2,0},{4,2},{6,4},{8,6},{10,8},{12,10},{14,12},{16,14},{18,... | collective-permute-start | bytes 1572872 | tf_op jit(solution)/shard_map/ppermute | solution.py:20
  108.0 2.1 multiply_convert_fusion.1
  110.1 3.8 %fusion.58 = f32[16,256,128]{1,2,0:T(8,128)} fusion(bf16[16,256,256]{2,1,0:T(8,128)(2,1)} %multiply_convert_fusion.1, bf16[256,16,128]{0,2,1:T(8,128)(2,1)S(1)} %bitcast.181), kind=kOutput, calls=%fused_computation.186 | convolution fusion | flops 268435456 | bytes 5242880 | tf_op jit(solution)/shard_map/hts,shd->thd/dot_general | solution.py:74
  113.9 3.4 %collective-permute-done.12 = bf16[128,2048]{1,0:T(8,128)(2,1)} collective-permute-done((bf16[128,2048]{1,0:T(8,128)(2,1)}, bf16[128,2048]{1,0:T(8,128)(2,1)}, u32[]{:S(2)}, u32[]{:S(2)}) %collective-permute-start.12) | collective-permute-done | bytes 524320 | tf_op jit(solution)/shard_map/ppermute | solution.py:20
  117.3 4.8 %collective-permute-start.13 = (bf16[128,2048]{1,0:T(8,128)(2,1)}, bf16[128,2048]{1,0:T(8,128)(2,1)}, u32[]{:S(2)}, u32[]{:S(2)}) collective-permute-start(bf16[128,2048]{1,0:T(8,128)(2,1)} %collective-permute-done.12), channel_id=1, source_target_pairs={{0,30},{2,0},{4,2},{6,4},{8,6},{10,8},{12,10},{14,12},{16,14},{18,... | collective-permute-start | bytes 1572872 | tf_op jit(solution)/shard_map/ppermute | solution.py:20
  122.3 2.6 fusion.5
  124.9 5.6 %multiply_convert_fusion = bf16[2048,2048]{1,0:T(8,128)(2,1)} fusion(bf16[256,2048]{0,1:T(8,128)(2,1)S(1)} %bitcast.201, bf16[1,256,2048]{2,1,0:T(8,128)(2,1)S(1)} %copy-done), kind=kOutput, calls=%fused_computation | convolution fusion | flops 2155872256 | bytes 10485760 | tf_op jit(solution)/shard_map/dot_general | solution.py:82
  130.6 4.7 %collective-permute-start.14 = (bf16[128,2048]{1,0:T(8,128)(2,1)}, bf16[128,2048]{1,0:T(8,128)(2,1)S(1)}, u32[]{:S(2)}, u32[]{:S(2)}) collective-permute-start(bf16[128,2048]{1,0:T(8,128)(2,1)} %collective-permute-done.13), channel_id=1, source_target_pairs={{0,30},{2,0},{4,2},{6,4},{8,6},{10,8},{12,10},{14,12},{16,14},{18,... | collective-permute-start | bytes 1572872 | tf_op jit(solution)/shard_map/ppermute | solution.py:20
  136.3 1.2 constant_dynamic-update-slice_fusion.30
  140.9 1.2 constant_dynamic-update-slice_fusion.26
  152.2 1.2 constant_dynamic-update-slice_fusion.15
  165.6 2.5 fusion.2
  169.1 1.3 fusion.8
  170.4 6.6 %all-to-all-start.2 = ((bf16[16,128,128]{2,1,0:T(8,128)(2,1)}), bf16[16,128,128]{2,1,0:T(8,128)(2,1)}, u32[]{:S(2)}, u32[]{:S(2)}) async-start(bf16[16,128,128]{2,1,0:T(8,128)(2,1)} %fusion.8), calls=%async_computation.2 | async-start | bytes 1048576 | tf_op jit(solution)/shard_map/all_to_all | solution.py:29
  177.0 3.4 %multiply_convert_fusion.2 = bf16[16,256,256]{2,1,0:T(8,128)(2,1)} fusion(bf16[256,16,128]{0,2,1:T(8,128)(2,1)} %bitcast.193, bf16[256,16,128]{0,2,1:T(8,128)(2,1)S(1)} %bitcast.182, f32[256,256]{1,0:T(8,128)S(1)} %fusion.21), kind=kOutput, calls=%fused_computation.4 | convolution fusion | flops 270532608 | bytes 4456448 | tf_op jit(solution)/shard_map/the,she->hts/dot_general | solution.py:95
  180.3 3.7 %fusion.57 = f32[16,128,256]{2,1,0:T(8,128)} fusion(bf16[256,16,128]{0,2,1:T(8,128)(2,1)} %bitcast.194, bf16[16,256,256]{2,1,0:T(8,128)(2,1)} %multiply_convert_fusion.1), kind=kOutput, calls=%fused_computation.185 | convolution fusion | flops 268435456 | bytes 5242880 | tf_op jit(solution)/shard_map/hts,the->she/dot_general | solution.py:106
  184.0 16.1 %all-to-all-done.2 = bf16[16,128,128]{2,1,0:T(8,128)(2,1)} async-done(((bf16[16,128,128]{2,1,0:T(8,128)(2,1)}), bf16[16,128,128]{2,1,0:T(8,128)(2,1)}, u32[]{:S(2)}, u32[]{:S(2)}) %all-to-all-start.2) | async-done | bytes 524320 | tf_op jit(solution)/shard_map/all_to_all | solution.py:29
  202.5 11.0 %all-to-all-start.3 = ((bf16[16,128,128]{2,1,0:T(8,128)(2,1)}), bf16[16,128,128]{2,1,0:T(8,128)(2,1)}, u32[]{:S(2)}, u32[]{:S(2)}) async-start(bf16[16,128,128]{2,1,0:T(8,128)(2,1)} %bitcast.203), calls=%async_computation.3 | async-start | bytes 1048576 | tf_op jit(solution)/shard_map/all_to_all | solution.py:37
  213.6 3.8 %fusion.12 = f32[16,256,128]{1,2,0:T(8,128)} fusion(bf16[16,256,256]{2,1,0:T(8,128)(2,1)} %multiply_convert_fusion.2, bf16[256,16,128]{2,1,0:T(8,128)(2,1)S(1)} %bitcast.186), kind=kOutput, calls=%fused_computation.19 | convolution fusion | flops 268435456 | bytes 5242880 | tf_op jit(solution)/shard_map/hts,shd->thd/dot_general | solution.py:98
  217.4 36.6 %reduce-scatter.3.cloned.1.call-done = bf16[128,2048]{1,0:T(8,128)(2,1)} async-done(((bf16[2048,2048]{1,0:T(8,128)(2,1)}), bf16[128,2048]{1,0:T(8,128)(2,1)}) %reduce-scatter.3.cloned.1.call-update) | async-done | bytes 524304 | tf_op jit(solution)/shard_map/reduce_scatter | solution.py:79
  254.0 3.5 %fusion.7 = bf16[256,16,128]{0,2,1:T(8,128)(2,1)} fusion(f32[16,256,128]{1,2,0:T(8,128)} %fusion.12, bf16[16,128,128]{2,1,0:T(8,128)(2,1)} %all-to-all-done.1, bf16[256,16,128]{0,2,1:T(8,128)(2,1)} %bitcast.195), kind=kOutput, calls=%fused_computation.11 | convolution fusion | flops 135266304 | bytes 4718592 | tf_op jit(solution)/shard_map/the,hde->thd/dot_general | solution.py:99
  257.4 2.3 copy.26
  259.7 3.8 %fusion.16 = f32[16,256,128]{1,2,0:T(8,128)} fusion(bf16[16,256,256]{2,1,0:T(8,128)(2,1)} %multiply_convert_fusion.2, bf16[256,16,128]{2,1,0:T(8,128)(2,1)} %bitcast.190), kind=kOutput, calls=%fused_computation.23 | convolution fusion | flops 268435456 | bytes 5242880 | tf_op jit(solution)/shard_map/hts,thd->shd/dot_general | solution.py:102
  263.5 3.2 %add_convert_fusion = bf16[16,128,256]{2,1,0:T(8,128)(2,1)} fusion(f32[16,128,256]{2,1,0:T(8,128)} %fusion.57, bf16[16,128,128]{2,1,0:T(8,128)(2,1)} %all-to-all-done.3, bf16[256,16,128]{2,1,0:T(8,128)(2,1)S(1)} %bitcast.187), kind=kOutput, calls=%fused_computation.12 | convolution fusion | flops 135266304 | bytes 4718592 | tf_op jit(solution)/shard_map/shd,hde->she/dot_general | solution.py:107
  266.8 2.3 copy.28
  269.0 2.2 fusion.6
  271.2 1.4 copy.27
  272.7 1.8 convert_element_type.208
  (107 shorter events, 42.3 us)
Async XLA Ops:
  7.2 117.7 %copy-start = (bf16[1,256,2048]{2,1,0:T(8,128)(2,1)S(1)}, bf16[1,256,2048]{2,1,0:T(8,128)(2,1)}, u32[]{:S(2)}) copy-start(bf16[1,256,2048]{2,1,0:T(8,128)(2,1)} %param.8) | copy-start | bytes 3145732
  11.5 32.9 %all-to-all-start = ((bf16[16,128,128]{2,1,0:T(8,128)(2,1)}), bf16[16,128,128]{2,1,0:T(8,128)(2,1)}, u32[]{:S(2)}, u32[]{:S(2)}) async-start(bf16[16,128,128]{2,1,0:T(8,128)(2,1)} %convolution_convert_fusion.1), calls=%async_computation | async-start | bytes 1048576 | tf_op jit(solution)/shard_map/all_to_all | solution.py:29
  28.4 0.8 copy-start.4
  28.4 11.6 %collective-permute-start = (bf16[128,2048]{1,0:T(8,128)(2,1)S(1)}, bf16[128,2048]{1,0:T(8,128)(2,1)}, u32[]{:S(2)}, u32[]{:S(2)}) collective-permute-start(bf16[128,2048]{1,0:T(8,128)(2,1)S(1)} %all_gather.3), channel_id=1, source_target_pairs={{0,2},{2,4},{4,6},{6,8},{8,10},{10,12},{12,14},{14,16},{16,18},{18... | collective-permute-start | bytes 1572872 | tf_op jit(solution)/shard_map/ppermute | solution.py:18
  29.2 13.4 %collective-permute-start.8 = (bf16[128,2048]{1,0:T(8,128)(2,1)S(1)}, bf16[128,2048]{1,0:T(8,128)(2,1)}, u32[]{:S(2)}, u32[]{:S(2)}) collective-permute-start(bf16[128,2048]{1,0:T(8,128)(2,1)S(1)} %all_gather.3), channel_id=1, source_target_pairs={{0,30},{2,0},{4,2},{6,4},{8,6},{10,8},{12,10},{14,12},{16,14},{18,... | collective-permute-start | bytes 1572872 | tf_op jit(solution)/shard_map/ppermute | solution.py:20
  40.0 11.7 %collective-permute-start.1 = (bf16[128,2048]{1,0:T(8,128)(2,1)}, bf16[128,2048]{1,0:T(8,128)(2,1)}, u32[]{:S(2)}, u32[]{:S(2)}) collective-permute-start(bf16[128,2048]{1,0:T(8,128)(2,1)} %collective-permute-done), channel_id=1, source_target_pairs={{0,2},{2,4},{4,6},{6,8},{8,10},{10,12},{12,14},{14,16},{16,18},{18... | collective-permute-start | bytes 1572872 | tf_op jit(solution)/shard_map/ppermute | solution.py:18
  42.6 24.5 %collective-permute-start.9 = (bf16[128,2048]{1,0:T(8,128)(2,1)}, bf16[128,2048]{1,0:T(8,128)(2,1)}, u32[]{:S(2)}, u32[]{:S(2)}) collective-permute-start(bf16[128,2048]{1,0:T(8,128)(2,1)} %collective-permute-done.8), channel_id=1, source_target_pairs={{0,30},{2,0},{4,2},{6,4},{8,6},{10,8},{12,10},{14,12},{16,14},{18,... | collective-permute-start | bytes 1572872 | tf_op jit(solution)/shard_map/ppermute | solution.py:20
  51.7 11.5 %collective-permute-start.2 = (bf16[128,2048]{1,0:T(8,128)(2,1)}, bf16[128,2048]{1,0:T(8,128)(2,1)S(1)}, u32[]{:S(2)}, u32[]{:S(2)}) collective-permute-start(bf16[128,2048]{1,0:T(8,128)(2,1)} %collective-permute-done.1), channel_id=1, source_target_pairs={{0,2},{2,4},{4,6},{6,8},{8,10},{10,12},{12,14},{14,16},{16,18},{18... | collective-permute-start | bytes 1572872 | tf_op jit(solution)/shard_map/ppermute | solution.py:18
  63.2 31.6 %copy-start.6 = (bf16[128,2048]{1,0:T(8,128)(2,1)}, bf16[128,2048]{1,0:T(8,128)(2,1)S(1)}, u32[]{:S(2)}) copy-start(bf16[128,2048]{1,0:T(8,128)(2,1)S(1)} %collective-permute-done.2) | copy-start | bytes 1572868
  63.2 11.4 %collective-permute-start.3 = (bf16[128,2048]{1,0:T(8,128)(2,1)S(1)}, bf16[128,2048]{1,0:T(8,128)(2,1)S(1)}, u32[]{:S(2)}, u32[]{:S(2)}) collective-permute-start(bf16[128,2048]{1,0:T(8,128)(2,1)S(1)} %collective-permute-done.2), channel_id=1, source_target_pairs={{0,2},{2,4},{4,6},{6,8},{8,10},{10,12},{12,14},{14,16},{16,18},{18... | collective-permute-start | bytes 1572872 | tf_op jit(solution)/shard_map/ppermute | solution.py:18
  67.1 14.1 %collective-permute-start.10 = (bf16[128,2048]{1,0:T(8,128)(2,1)}, bf16[128,2048]{1,0:T(8,128)(2,1)}, u32[]{:S(2)}, u32[]{:S(2)}) collective-permute-start(bf16[128,2048]{1,0:T(8,128)(2,1)} %collective-permute-done.9), channel_id=1, source_target_pairs={{0,30},{2,0},{4,2},{6,4},{8,6},{10,8},{12,10},{14,12},{16,14},{18,... | collective-permute-start | bytes 1572872 | tf_op jit(solution)/shard_map/ppermute | solution.py:20
  74.6 20.2 %copy-start.8 = (bf16[128,2048]{1,0:T(8,128)(2,1)}, bf16[128,2048]{1,0:T(8,128)(2,1)S(1)}, u32[]{:S(2)}) copy-start(bf16[128,2048]{1,0:T(8,128)(2,1)S(1)} %collective-permute-done.3) | copy-start | bytes 1572868
  74.6 11.4 %collective-permute-start.4 = (bf16[128,2048]{1,0:T(8,128)(2,1)S(1)}, bf16[128,2048]{1,0:T(8,128)(2,1)}, u32[]{:S(2)}, u32[]{:S(2)}) collective-permute-start(bf16[128,2048]{1,0:T(8,128)(2,1)S(1)} %collective-permute-done.3), channel_id=1, source_target_pairs={{0,2},{2,4},{4,6},{6,8},{8,10},{10,12},{12,14},{14,16},{16,18},{18... | collective-permute-start | bytes 1572872 | tf_op jit(solution)/shard_map/ppermute | solution.py:18
  81.2 22.4 %collective-permute-start.11 = (bf16[128,2048]{1,0:T(8,128)(2,1)}, bf16[128,2048]{1,0:T(8,128)(2,1)}, u32[]{:S(2)}, u32[]{:S(2)}) collective-permute-start(bf16[128,2048]{1,0:T(8,128)(2,1)} %collective-permute-done.10), channel_id=1, source_target_pairs={{0,30},{2,0},{4,2},{6,4},{8,6},{10,8},{12,10},{14,12},{16,14},{18,... | collective-permute-start | bytes 1572872 | tf_op jit(solution)/shard_map/ppermute | solution.py:20
  86.0 22.0 %collective-permute-start.5 = (bf16[128,2048]{1,0:T(8,128)(2,1)}, bf16[128,2048]{1,0:T(8,128)(2,1)}, u32[]{:S(2)}, u32[]{:S(2)}) collective-permute-start(bf16[128,2048]{1,0:T(8,128)(2,1)} %collective-permute-done.4), channel_id=1, source_target_pairs={{0,2},{2,4},{4,6},{6,8},{8,10},{10,12},{12,14},{14,16},{16,18},{18... | collective-permute-start | bytes 1572872 | tf_op jit(solution)/shard_map/ppermute | solution.py:18
  94.8 27.4 %all-to-all-start.1 = ((bf16[16,128,128]{2,1,0:T(8,128)(2,1)}), bf16[16,128,128]{2,1,0:T(8,128)(2,1)}, u32[]{:S(2)}, u32[]{:S(2)}) async-start(bf16[16,128,128]{2,1,0:T(8,128)(2,1)} %bitcast.202), calls=%async_computation.1 | async-start | bytes 1048576 | tf_op jit(solution)/shard_map/all_to_all | solution.py:37
  102.1 151.9 %reduce-scatter.3.cloned.1.call-start = ((), (), s32[]{:S(2)}) async-start(), calls=%async_computation.6 | async-start | bytes 8912896 | tf_op jit(solution)/shard_map/reduce_scatter | solution.py:79
  103.6 4.4 %copy-start.1 = (bf16[32,8,16,128]{3,2,1,0:T(8,128)(2,1)}, bf16[32,8,16,128]{3,2,1,0:T(8,128)(2,1)S(1)}, u32[]{:S(2)}) copy-start(bf16[32,8,16,128]{3,2,1,0:T(8,128)(2,1)S(1)} %copy.36) | copy-start | bytes 3145732
  103.6 13.6 %collective-permute-start.12 = (bf16[128,2048]{1,0:T(8,128)(2,1)}, bf16[128,2048]{1,0:T(8,128)(2,1)}, u32[]{:S(2)}, u32[]{:S(2)}) collective-permute-start(bf16[128,2048]{1,0:T(8,128)(2,1)} %collective-permute-done.11), channel_id=1, source_target_pairs={{0,30},{2,0},{4,2},{6,4},{8,6},{10,8},{12,10},{14,12},{16,14},{18,... | collective-permute-start | bytes 1572872 | tf_op jit(solution)/shard_map/ppermute | solution.py:20
  108.0 14.3 %collective-permute-start.6 = (bf16[128,2048]{1,0:T(8,128)(2,1)}, bf16[128,2048]{1,0:T(8,128)(2,1)}, u32[]{:S(2)}, u32[]{:S(2)}) collective-permute-start(bf16[128,2048]{1,0:T(8,128)(2,1)} %collective-permute-done.5), channel_id=1, source_target_pairs={{0,2},{2,4},{4,6},{6,8},{8,10},{10,12},{12,14},{14,16},{16,18},{18... | collective-permute-start | bytes 1572872 | tf_op jit(solution)/shard_map/ppermute | solution.py:18
  117.3 13.3 %collective-permute-start.13 = (bf16[128,2048]{1,0:T(8,128)(2,1)}, bf16[128,2048]{1,0:T(8,128)(2,1)}, u32[]{:S(2)}, u32[]{:S(2)}) collective-permute-start(bf16[128,2048]{1,0:T(8,128)(2,1)} %collective-permute-done.12), channel_id=1, source_target_pairs={{0,30},{2,0},{4,2},{6,4},{8,6},{10,8},{12,10},{14,12},{16,14},{18,... | collective-permute-start | bytes 1572872 | tf_op jit(solution)/shard_map/ppermute | solution.py:20
  122.3 13.0 %collective-permute-start.7 = (bf16[128,2048]{1,0:T(8,128)(2,1)}, bf16[128,2048]{1,0:T(8,128)(2,1)}, u32[]{:S(2)}, u32[]{:S(2)}) collective-permute-start(bf16[128,2048]{1,0:T(8,128)(2,1)} %collective-permute-done.6), channel_id=1, source_target_pairs={{0,2},{2,4},{4,6},{6,8},{8,10},{10,12},{12,14},{14,16},{16,18},{18... | collective-permute-start | bytes 1572872 | tf_op jit(solution)/shard_map/ppermute | solution.py:18
  130.5 26.2 %copy-start.9 = (bf16[128,2048]{1,0:T(8,128)(2,1)S(1)}, bf16[128,2048]{1,0:T(8,128)(2,1)}, u32[]{:S(2)}) copy-start(bf16[128,2048]{1,0:T(8,128)(2,1)} %copy-done.8) | copy-start | bytes 1572868
  130.5 26.2 %copy-start.7 = (bf16[128,2048]{1,0:T(8,128)(2,1)S(1)}, bf16[128,2048]{1,0:T(8,128)(2,1)}, u32[]{:S(2)}) copy-start(bf16[128,2048]{1,0:T(8,128)(2,1)} %copy-done.6) | copy-start | bytes 1572868
  130.5 28.4 %copy-start.5 = (bf16[128,2048]{1,0:T(8,128)(2,1)S(1)}, bf16[128,2048]{1,0:T(8,128)(2,1)}, u32[]{:S(2)}) copy-start(bf16[128,2048]{1,0:T(8,128)(2,1)} %copy-done.4) | copy-start | bytes 1572868
  130.6 21.5 %collective-permute-start.14 = (bf16[128,2048]{1,0:T(8,128)(2,1)}, bf16[128,2048]{1,0:T(8,128)(2,1)S(1)}, u32[]{:S(2)}, u32[]{:S(2)}) collective-permute-start(bf16[128,2048]{1,0:T(8,128)(2,1)} %collective-permute-done.13), channel_id=1, source_target_pairs={{0,30},{2,0},{4,2},{6,4},{8,6},{10,8},{12,10},{14,12},{16,14},{18,... | collective-permute-start | bytes 1572872 | tf_op jit(solution)/shard_map/ppermute | solution.py:20
  152.2 17.0 %copy-start.2 = (bf16[32,8,16,128]{3,2,1,0:T(8,128)(2,1)S(1)}, bf16[32,8,16,128]{3,2,1,0:T(8,128)(2,1)}, u32[]{:S(2)}) copy-start(bf16[32,8,16,128]{3,2,1,0:T(8,128)(2,1)} %copy-done.1) | copy-start | bytes 3145732
  168.2 1.0 copy-start.3
  170.4 29.7 %all-to-all-start.2 = ((bf16[16,128,128]{2,1,0:T(8,128)(2,1)}), bf16[16,128,128]{2,1,0:T(8,128)(2,1)}, u32[]{:S(2)}, u32[]{:S(2)}) async-start(bf16[16,128,128]{2,1,0:T(8,128)(2,1)} %fusion.8), calls=%async_computation.2 | async-start | bytes 1048576 | tf_op jit(solution)/shard_map/all_to_all | solution.py:29
  201.7 0.8 copy-start.10
  202.5 61.0 %all-to-all-start.3 = ((bf16[16,128,128]{2,1,0:T(8,128)(2,1)}), bf16[16,128,128]{2,1,0:T(8,128)(2,1)}, u32[]{:S(2)}, u32[]{:S(2)}) async-start(bf16[16,128,128]{2,1,0:T(8,128)(2,1)} %bitcast.203), calls=%async_computation.3 | async-start | bytes 1048576 | tf_op jit(solution)/shard_map/all_to_all | solution.py:37
  213.5 59.1 %reduce-scatter.5.cloned.1.call-start = ((), (), s32[]{:S(2)}) async-start(), calls=%async_computation.7 | async-start | bytes 786432 | tf_op jit(solution)/shard_map/reduce_scatter | solution.py:90
Sparse Core Ops, SparseCore 0:
  130.6 123.2 reduce-scatter.2
  256.2 14.3 reduce-scatter.4
